TPU v7x, 256 devices: a whole 4x4x8 slice. The times are simulated.
256 devices in a mesh: dp: 32 (over x, z), tensor: 8 (over y, core).
Axes of the slice: x: 4, y: 4, z: 8, core: 2. Of those that a mesh axis runs over, the one named last changes fastest.
Arguments:
- tubelets: bfloat16 [1024, 32, 4096], P('dp', 'tensor'), may hold values from -6 to 6
- keep_index: int32 [1024, 32], P('dp', 'tensor'), may hold values from -1 to 31, as said below
- dest_row: int32 [1024, 32], P('dp', 'tensor'), may hold values from -1 to 31, as said below
- dest_slot: int32 [1024, 32], P('dp', 'tensor'), may hold values from -1 to 1023, as said below
- segment: int32 [32, 1024], P('dp'), may hold values from -1 to 1023, as said below
- ln_gain: bfloat16 [4096], replicated, may hold values from 0.25 to 1.75
- w_query: bfloat16 [4096, 3072], P('dp', 'tensor')
- w_key: bfloat16 [4096, 3072], P('dp', 'tensor')
- w_value: bfloat16 [4096, 3072], P('dp', 'tensor'), may hold values from -0.09375 to 0.09375
Outputs:
- attended: bfloat16 [32, 1024, 3072], P('dp', None, 'tensor')
Inputs may be any that keep to these rules, and one draw needn't show every extreme that they name: `keep_index`: entry e of a clip's list belongs to tensor index e // 4 and, when kept, names a tubelet of that index's share, each at most once; -1 marks a dropped entry. Each share keeps 1 to 4 tubelets. `dest_row`: -1 exactly where keep_index is -1. A clip goes whole to one row; each row receives exactly one clip from each dp index, so at most 4 kept tubelets go from one device to one row; some dp index sends that many to every row. `dest_slot`: -1 exactly where keep_index is -1. A kept tubelet on tensor index j lands in slots j * 128 to (j + 1) * 128 - 1; no two kept tubelets share a row and a slot; some row has all its slots filled. `segment`: the clip whose tubelet fills each slot, clips numbered in the order of the tubelets array; -1 for an empty slot. Agrees with dest_row and dest_slot.
All inputs are finite; a program needn't handle non-finite values.
Results may differ from a plain program's by a relative error of at most 0.0082.
Values may be sent and summed in bfloat16 or wider, within the bound.
A program may use at most 64 MiB of HBM per device.

v0:
```python
import jax
import jax.numpy as jnp
from jax import lax
from jax.sharding import PartitionSpec as P

HS = 128


block_rows = 512


def layer_norm(values_in, ln_gain):
    floats = values_in.astype(jnp.float32)
    average = jnp.mean(floats, axis=-1, keepdims=True)
    centred = floats - average
    variance = jnp.mean(centred * centred, axis=-1, keepdims=True)
    return (centred * lax.rsqrt(variance + 1e-06) * ln_gain.astype(jnp.float32)).astype(
        jnp.bfloat16
    )


def bucket_targets(row_ids, is_kept, n_buckets, capacity):
    matches = (row_ids[:, None] == jnp.arange(n_buckets, dtype=jnp.int32)[None, :]).astype(
        jnp.int32
    )
    earlier = jnp.cumsum(matches, axis=0) - matches
    ranking = jnp.sum(earlier * matches, axis=1)
    return jnp.where(is_kept, row_ids * capacity + ranking, -1)


def invert(targets, first_vals, second_vals, count):
    matches = targets[None, :] == jnp.arange(count, dtype=jnp.int32)[:, None]
    present = jnp.any(matches, axis=1)
    first_pick = jnp.sum(jnp.where(matches, first_vals[None, :], 0), axis=1)
    second_pick = jnp.sum(jnp.where(matches, second_vals[None, :], 0), axis=1)
    return (present, first_pick, second_pick)


def pack_send(flat_rows, source_ids, row_ids, slot_ids, is_kept, n_buckets):
    entries = source_ids.shape[0]
    capacity = entries // n_buckets
    targets = bucket_targets(row_ids, is_kept, n_buckets, capacity)
    present, source_pick, slot_pick = invert(targets, source_ids, slot_ids, entries)
    send_rows = jnp.where(
        present[:, None], jnp.take(flat_rows, source_pick, axis=0), jnp.zeros((), flat_rows.dtype)
    )
    send_slots = jnp.where(present, slot_pick, -1)
    return (
        send_rows.reshape(n_buckets, capacity, flat_rows.shape[1]),
        send_slots.reshape(n_buckets, capacity),
    )


def place_rows(recv_rows, recv_slots, slot_count):
    flat_rows = recv_rows.reshape(-1, recv_rows.shape[-1])
    flat_slots = recv_slots.reshape(-1)
    positions = jnp.arange(flat_slots.shape[0], dtype=jnp.int32)
    present, picked, ignored = invert(flat_slots, positions, positions, slot_count)
    return jnp.where(
        present[:, None], jnp.take(flat_rows, picked, axis=0), jnp.zeros((), flat_rows.dtype)
    )


def attend(query_rows, key_rows, value_rows, seg_query, seg_key):
    scores = jnp.einsum("qhd,khd->hqk", query_rows, key_rows, preferred_element_type=jnp.float32)
    allowed = (seg_query[:, None] == seg_key[None, :]) & (seg_key[None, :] >= 0)
    masked = jnp.where(allowed[None], scores, -1e30)
    largest = jnp.max(masked, axis=-1, keepdims=True)
    weights = jnp.where(allowed[None], jnp.exp(masked - largest), 0.0)
    totals = jnp.sum(weights, axis=-1, keepdims=True)
    totals = jnp.where(totals > 0, totals, 1.0)
    weights_bf = (weights / totals).astype(jnp.bfloat16)
    mixed = jnp.einsum("hqk,khd->qhd", weights_bf, value_rows, preferred_element_type=jnp.float32)
    return mixed.astype(jnp.bfloat16)


def body(tubelets, keep_index, dest_row, dest_slot, segment, ln_gain, w_query, w_key, w_value):
    n_rows = lax.axis_size("dp")
    clip_count, share_len, width = tubelets.shape
    seg_ids = segment.reshape(-1)
    row_len = seg_ids.shape[0]
    tok_rows = row_len // lax.axis_size("tensor")
    width_cols = w_query.shape[1]
    heads_local = width_cols // HS
    column = lax.axis_index("tensor")
    is_kept = (keep_index >= 0).reshape(-1)
    local_ids = jnp.maximum(keep_index - column * share_len, 0)
    source_ids = (jnp.arange(clip_count, dtype=jnp.int32)[:, None] * share_len + local_ids).reshape(
        -1
    )
    local_slots = (dest_slot - column * tok_rows).reshape(-1)
    send_rows, send_slots = pack_send(
        tubelets.reshape(-1, width), source_ids, dest_row.reshape(-1), local_slots, is_kept, n_rows
    )
    recv_rows, recv_slots = (
        lax.all_to_all(send_rows, "dp", split_axis=0, concat_axis=0, tiled=True),
        lax.all_to_all(send_slots, "dp", split_axis=0, concat_axis=0, tiled=True),
    )
    normed_own = layer_norm(place_rows(recv_rows, recv_slots, tok_rows), ln_gain)
    normed_row = lax.all_gather(normed_own, "tensor", axis=0, tiled=True)
    pieces_in = (
        lax.all_gather(w_query, "dp", axis=0, tiled=True),
        lax.all_gather(w_key, "dp", axis=0, tiled=True),
        lax.all_gather(w_value, "dp", axis=0, tiled=True),
    )
    query_sum, key_sum, value_sum = tuple(
        (jnp.dot(normed_row, piece_w, preferred_element_type=jnp.float32) for piece_w in pieces_in)
    )
    query_rows = (query_sum * HS ** (-0.5)).astype(jnp.bfloat16)
    key_rows = key_sum.astype(jnp.bfloat16).reshape(row_len, heads_local, HS)
    value_rows = value_sum.astype(jnp.bfloat16).reshape(row_len, heads_local, HS)
    blocks = row_len // block_rows
    query_blocks = query_rows.reshape(blocks, block_rows, heads_local, HS)
    seg_blocks = seg_ids.reshape(blocks, block_rows)
    mixed = lax.map(
        lambda pair_in: attend(pair_in[0], key_rows, value_rows, pair_in[1], seg_ids),
        (query_blocks, seg_blocks),
    )
    return mixed.reshape(1, row_len, width_cols)


def solution(mesh):
    return jax.shard_map(
        body,
        mesh=mesh,
        in_specs=(
            P("dp", "tensor", None),
            P("dp", "tensor"),
            P("dp", "tensor"),
            P("dp", "tensor"),
            P("dp", None),
            P(),
            P("dp", "tensor"),
            P("dp", "tensor"),
            P("dp", "tensor"),
        ),
        out_specs=P("dp", None, "tensor"),
        check_vma=False,
    )
```

profile of v0, /device:TPU:16, one launch (start us, length us, event | category | flops | bytes accessed | tf_op | source)
XLA Modules:
  0.0 343.8 jit_solution(8539267349982979860)
XLA Ops:
  7.3 0.8 copy.40
  12.2 11.3 %all-to-all-start = ((s32[32,1,4]{2,1,0:T(1,128)}), s32[32,1,4]{2,1,0:T(1,128)S(1)}, u32[]{:S(2)}, u32[]{:S(2)}) async-start(s32[32,1,4]{2,1,0:T(1,128)} %bitcast.5), calls=%async_computation | async-start | bytes 32768 | tf_op jit(solution)/shard_map/all_to_all | solution.py:97
  23.6 1.4 reshape.154
  25.0 1.2 gather_fusion
  26.4 1.2 reshape.155
  27.6 5.7 %all-to-all-done = s32[32,1,4]{2,1,0:T(1,128)S(1)} async-done(((s32[32,1,4]{2,1,0:T(1,128)}), s32[32,1,4]{2,1,0:T(1,128)S(1)}, u32[]{:S(2)}, u32[]{:S(2)}) %all-to-all-start) | async-done | bytes 544 | tf_op jit(solution)/shard_map/all_to_all | solution.py:97
  33.3 4.1 %all-to-all-start.1 = ((bf16[32,4,4096]{2,1,0:T(4,128)(2,1)}), bf16[32,4,4096]{2,1,0:T(4,128)(2,1)S(1)}, u32[]{:S(2)}, u32[]{:S(2)}) async-start(bf16[32,4,4096]{2,1,0:T(4,128)(2,1)} %reshape.155), calls=%async_computation.1 | async-start | bytes 2097152 | tf_op jit(solution)/shard_map/all_to_all | solution.py:96
  39.1 28.2 %all-to-all-done.1 = bf16[32,4,4096]{2,1,0:T(4,128)(2,1)S(1)} async-done(((bf16[32,4,4096]{2,1,0:T(4,128)(2,1)}), bf16[32,4,4096]{2,1,0:T(4,128)(2,1)S(1)}, u32[]{:S(2)}, u32[]{:S(2)}) %all-to-all-start.1) | async-done | bytes 1048608 | tf_op jit(solution)/shard_map/all_to_all | solution.py:96
  67.5 1.2 gather_fusion.1
  69.7 1.5 fusion.32
  73.2 21.5 %all-gather.7.cloned.1.call-done = bf16[4096,384]{1,0:T(8,128)(2,1)} async-done(((bf16[128,384]{1,0:T(8,128)(2,1)}), bf16[4096,384]{1,0:T(8,128)(2,1)}) %all-gather.7.cloned.1.call-update) | async-done | bytes 3145744 | tf_op jit(solution)/shard_map/all_gather | solution.py:102
  94.7 49.7 %all-gather.5.cloned.1.call-done = bf16[1024,4096]{1,0:T(8,128)(2,1)} async-done(((bf16[128,4096]{1,0:T(8,128)(2,1)}), bf16[1024,4096]{1,0:T(8,128)(2,1)}) %all-gather.5.cloned.1.call-update) | async-done | bytes 8388624 | tf_op jit(solution)/shard_map/all_gather | solution.py:100
  144.4 8.8 %multiply_convert_fusion = bf16[1024,384]{1,0:T(8,128)(2,1)S(1)} fusion(bf16[1024,4096]{1,0:T(8,128)(2,1)} %all-gather.5.cloned.1.call-done, bf16[4096,384]{1,0:T(8,128)(2,1)} %all-gather.7.cloned.1.call-done), kind=kOutput, calls=%fused_computation.33 | convolution fusion | flops 3222011904 | bytes 12320768 | tf_op jit(solution)/shard_map/dot_general | solution.py:107
  153.7 74.0 %all-gather.9.cloned.1.call-done = bf16[4096,384]{1,0:T(8,128)(2,1)} async-done(((bf16[128,384]{1,0:T(8,128)(2,1)}), bf16[4096,384]{1,0:T(8,128)(2,1)}) %all-gather.9.cloned.1.call-update) | async-done | bytes 3145744 | tf_op jit(solution)/shard_map/all_gather | solution.py:103
  227.7 7.7 %convolution_convert_fusion.1 = bf16[1024,384]{0,1:T(8,128)(2,1)S(1)} fusion(bf16[1024,4096]{1,0:T(8,128)(2,1)} %all-gather.5.cloned.1.call-done, bf16[4096,384]{1,0:T(8,128)(2,1)} %all-gather.9.cloned.1.call-done), kind=kOutput, calls=%fused_computation.35 | convolution fusion | flops 3221618688 | bytes 12320768 | tf_op jit(solution)/shard_map/dot_general | solution.py:107
  235.8 70.4 %all-gather.11.cloned.1.call-done = bf16[4096,384]{1,0:T(8,128)(2,1)} async-done(((bf16[128,384]{1,0:T(8,128)(2,1)}), bf16[4096,384]{1,0:T(8,128)(2,1)}) %all-gather.11.cloned.1.call-update) | async-done | bytes 3145744 | tf_op jit(solution)/shard_map/all_gather | solution.py:104
  306.2 7.7 %convolution_convert_fusion = bf16[1024,384]{0,1:T(8,128)(2,1)S(1)} fusion(bf16[1024,4096]{1,0:T(8,128)(2,1)} %all-gather.5.cloned.1.call-done, bf16[4096,384]{1,0:T(8,128)(2,1)} %all-gather.11.cloned.1.call-done), kind=kOutput, calls=%fused_computation.34 | convolution fusion | flops 3221618688 | bytes 12320768 | tf_op jit(solution)/shard_map/dot_general | solution.py:107
  314.0 1.2 copy.47
  315.1 20.0 %while.10 = (s32[]{:T(128)}, bf16[2,512,3,128]{3,1,2,0:T(8,128)(2,1)S(1)}, s32[2,512]{1,0:T(2,128)S(1)}, s32[1,1024]{1,0:T(1,128)S(1)}, bf16[2,512,3,128]{3,1,2,...) while((s32[]{:T(128)}, ...), condition=%wide.region_12.14_spmd, body=%wide.region_9.13_spmd.sunk | while | flops 815993856 | bytes 16558177 | solution.py:115
  315.6 5.4 %fusion.58 = (f32[3,512]{1,0:T(4,128)S(1)}, f32[3,512,1024]{2,1,0:T(8,128)}) fusion(pred[512,1024]{1,0:T(8,128)(4,1)S(1)} %compare_and_fusion.4, bf16[1024,3,128]{2,0,1:T(8,128)(2,1)S(1)} %get-tuple-element.160, bf16[2,512,3,128]{3,1,2,0:T(8,128)(2,1)S(1)} %get-tuple-element.159, s32[]{:T(128)} %get-tuple-element.147), kind=kOutput, calls=%fused_computation.62.clone.1 | convolution fusion | flops 408945664 | bytes 8525828 | tf_op jit(solution)/shard_map/while/body/eval_jaxpr/sub | solution.py:69
  321.0 4.1 %fusion.59 = bf16[2,512,3,128]{3,1,2,0:T(8,128)(2,1)S(1)} fusion(bf16[2,512,3,128]{3,1,2,0:T(8,128)(2,1)S(1)} %get-tuple-element.148, s32[]{:T(128)} %get-tuple-element.147, bf16[1024,3,128]{2,0,1:T(8,128)(2,1)} %get-tuple-element.161, f32[3,512,1024]{2,1,0:T(8,128)} %get-tuple-element.137, f32[3,512]{1,0:T(4,128)S(1)} %compare_select_fusion.4), kind=kOutput, calls=%fused_computation.13.clone.1 | convolution fusion | flops 405995520 | bytes 7479300 | tf_op jit(solution)/shard_map/while/body/eval_jaxpr/hqk,khd->qhd/dot_general | solution.py:73
  325.6 5.4 %fusion.58 = (f32[3,512]{1,0:T(4,128)S(1)}, f32[3,512,1024]{2,1,0:T(8,128)}) fusion(pred[512,1024]{1,0:T(8,128)(4,1)S(1)} %compare_and_fusion.4, bf16[1024,3,128]{2,0,1:T(8,128)(2,1)S(1)} %get-tuple-element.160, bf16[2,512,3,128]{3,1,2,0:T(8,128)(2,1)S(1)} %get-tuple-element.159, s32[]{:T(128)} %get-tuple-element.147), kind=kOutput, calls=%fused_computation.62.clone.1 | convolution fusion | flops 408945664 | bytes 8525828 | tf_op jit(solution)/shard_map/while/body/eval_jaxpr/sub | solution.py:69
  331.0 4.1 %fusion.59 = bf16[2,512,3,128]{3,1,2,0:T(8,128)(2,1)S(1)} fusion(bf16[2,512,3,128]{3,1,2,0:T(8,128)(2,1)S(1)} %get-tuple-element.148, s32[]{:T(128)} %get-tuple-element.147, bf16[1024,3,128]{2,0,1:T(8,128)(2,1)} %get-tuple-element.161, f32[3,512,1024]{2,1,0:T(8,128)} %get-tuple-element.137, f32[3,512]{1,0:T(4,128)S(1)} %compare_select_fusion.4), kind=kOutput, calls=%fused_computation.13.clone.1 | convolution fusion | flops 405995520 | bytes 7479300 | tf_op jit(solution)/shard_map/while/body/eval_jaxpr/hqk,khd->qhd/dot_general | solution.py:73
  335.8 1.4 reshape.184
  (64 shorter events, 12.3 us)
Async XLA Ops:
  6.5 88.1 %all-gather.7.cloned.1.call-start = ((), (), s32[]{:S(2)}) async-start(), calls=%async_computation.3 | async-start | bytes 3244032 | tf_op jit(solution)/shard_map/all_gather | solution.py:102
  12.2 21.1 %all-to-all-start = ((s32[32,1,4]{2,1,0:T(1,128)}), s32[32,1,4]{2,1,0:T(1,128)S(1)}, u32[]{:S(2)}, u32[]{:S(2)}) async-start(s32[32,1,4]{2,1,0:T(1,128)} %bitcast.5), calls=%async_computation | async-start | bytes 32768 | tf_op jit(solution)/shard_map/all_to_all | solution.py:97
  26.2 11.3 %copy-start.1 = (bf16[4096]{0:T(1024)(128)(2,1)S(1)}, bf16[4096]{0:T(1024)(128)(2,1)}, u32[]{:S(2)}) copy-start(bf16[4096]{0:T(1024)(128)(2,1)} %param.18) | copy-start | bytes 24580
  33.3 34.0 %all-to-all-start.1 = ((bf16[32,4,4096]{2,1,0:T(4,128)(2,1)}), bf16[32,4,4096]{2,1,0:T(4,128)(2,1)S(1)}, u32[]{:S(2)}, u32[]{:S(2)}) async-start(bf16[32,4,4096]{2,1,0:T(4,128)(2,1)} %reshape.155), calls=%async_computation.1 | async-start | bytes 2097152 | tf_op jit(solution)/shard_map/all_to_all | solution.py:96
  37.4 107.0 %all-gather.5.cloned.1.call-start = ((), (), s32[]{:S(2)}) async-start(), calls=%async_computation.2 | async-start | bytes 9437184 | tf_op jit(solution)/shard_map/all_gather | solution.py:100
  68.7 3.8 %copy-start = (s32[1,1024]{1,0:T(1,128)S(1)}, s32[1,1024]{1,0:T(1,128)}, u32[]{:S(2)}) copy-start(s32[1,1024]{1,0:T(1,128)} %param.17) | copy-start | bytes 12292
  71.2 156.6 %all-gather.9.cloned.1.call-start = ((), (), s32[]{:S(2)}) async-start(), calls=%async_computation.4 | async-start | bytes 3244032 | tf_op jit(solution)/shard_map/all_gather | solution.py:103
  71.9 234.3 %all-gather.11.cloned.1.call-start = ((), (), s32[]{:S(2)}) async-start(), calls=%async_computation.5 | async-start | bytes 3244032 | tf_op jit(solution)/shard_map/all_gather | solution.py:104
Sparse Core Ops, SparseCore 0:
  9.9 84.7 all-gather.6
  96.5 47.8 all-gather.4
  147.0 80.6 all-gather.8
  230.2 76.0 all-gather.10
where the time goes:
time: 344 us
  waiting for transfers between devices  251 us (73%)
  matrix products  43.3 us (13%)
  starting transfers between devices  15.6 us (5%)
  between operations  13.4 us (4%)
  local copies, waits for them, and re-layouts  12.3 us (4%)
  other arithmetic  7.78 us (2%)
    all_gather x1, waiting for transfers between devices, body(): lax.all_gather(w_key, 'dp', axis=0, tiled=True)  74 us
    all_gather x1, waiting for transfers between devices, body(): lax.all_gather(w_value, 'dp', axis=0, tiled=True)  70.4 us
    all_gather x1, waiting for transfers between devices, body(): normed_row = lax.all_gather(normed_own, 'tensor', axis=0, tiled=True)  49.7 us
    all_to_all x1, waiting for transfers between devices, body(): lax.all_to_all(send_rows, 'dp', split_axis=0, concat_axis=0, tiled=True)  28.2 us
    dot_general x3, matrix products, body(): jnp.dot(normed_row, piece_w, preferred_element_type=jnp.float32)  24.2 us
    all_gather x1, waiting for transfers between devices, body(): lax.all_gather(w_query, 'dp', axis=0, tiled=True)  21.5 us
    all_to_all x1, starting transfers between devices, body(): lax.all_to_all(send_slots, 'dp', split_axis=0, concat_axis=0, tiled=True)  11.3 us
    sub x2, matrix products, attend(): weights = jnp.where(allowed[None], jnp.exp(masked - largest), 0.0)  10.8 us
  transfers between devices with their start and end apart: 6, of which 6 were waited for; matrix products, arithmetic and copies ran while one was open for 9% of the time, Pallas kernels for 0%

commit v1 on v0

v1 whole, which is shorter than its diff:
```python
import jax
import jax.numpy as jnp
from jax import lax
from jax.experimental import pallas as pl
from jax.experimental.pallas import tpu as pltpu
from jax.sharding import PartitionSpec as P

MESH = pl.DeviceIdType.MESH
F32 = jnp.float32
BF16 = jnp.bfloat16
HS = 128
NX, NZ, NY = 4, 8, 4
NDP, NT = NX * NZ, 2 * NY
KEEP = 4
HEADS = 3
BLK = 128

A_ROWS, A_PLUS = 48, 16
B_ROWS = BLK - A_ROWS
BZ_PLUS, BX_PLUS = 32, 32

W_KEYS = (
    [("ax", d, t) for t in (1, 2) for d in (0, 1)]
    + [("bz", d, t) for t in (1, 2, 3, 4) for d in (0, 1)]
    + [("az", d, t) for t in (1, 2, 3, 4) for d in (0, 1)]
    + [("bx", d, t) for t in (1, 2) for d in (0, 1)]
)
W_ID = {(h,) + key: h * len(W_KEYS) + n for h in range(HEADS) for n, key in enumerate(W_KEYS)}
Y_KEYS = ("p1", "m1", "p2", "m2", "own", "fp1", "fm1", "f2")
Y_ID = {(g, key): len(W_ID) + g * len(Y_KEYS) + n for g in range(NX) for n, key in enumerate(Y_KEYS)}
N_MSG = len(W_ID) + len(Y_ID)


def iota(shape, dim):
    return lax.broadcasted_iota(jnp.int32, shape, dim)


def one_hot(mask):
    return jnp.where(mask, 1.0, 0.0).astype(BF16)


def kernel(
    tub, keep, row, slot, seg, gain, wq, wk, wv, out,
    xn, snd, rcv, nrm, wall, qkv, att, bias, place, present,
    lsem, a2a_s, a2a_r, ss, rs,
):
    p_me, j_me = lax.axis_index("dp"), lax.axis_index("tensor")
    x, z = p_me // NZ, lax.rem(p_me, NZ)
    y, c = j_me // 2, lax.rem(j_me, 2)

    def wrap(v, n):
        return lax.rem(v + n, n)

    def dp_of(xx, zz):
        return {"dp": wrap(xx, NX) * NZ + wrap(zz, NZ)}

    def ten_of(yy, cc):
        return {"tensor": wrap(yy, NY) * 2 + cc}

    barrier = pltpu.get_barrier_semaphore()

    @pl.loop(1, NDP)
    def _(d):
        pl.semaphore_signal(
            barrier, inc=1, device_id={"dp": lax.rem(p_me + d, NDP)}, device_id_type=MESH
        )

    for dev in (ten_of(y + 1, c), ten_of(y - 1, c), ten_of(y, 1 - c)):
        pl.semaphore_signal(barrier, inc=1, device_id=dev, device_id_type=MESH)

    local = []
    for h in range(HEADS):
        for n, w in enumerate((wq, wk, wv)):
            cp = pltpu.make_async_copy(
                w.at[:, pl.ds(h * HS, HS)],
                wall.at[h, x, z, :, pl.ds(n * HS, HS)],
                lsem.at[h * 3 + n],
            )
            cp.start()
            local.append(cp)

    @pl.loop(0, BLK // 16)
    def _(i):
        at = pl.ds(pl.multiple_of(i * 16, 16), 16)
        v = tub[at, :].astype(F32)
        v = v - jnp.mean(v, axis=-1, keepdims=True)
        var = jnp.mean(v * v, axis=-1, keepdims=True)
        xn[at, :] = (v * lax.rsqrt(var + 1e-06) * gain[...].astype(F32)).astype(BF16)

    pl.semaphore_wait(barrier, NDP - 1 + 3)
    for cp in local:
        cp.wait()

    sent = []

    def copy(region, n, dev):
        return pltpu.make_async_remote_copy(
            src_ref=region, dst_ref=region, send_sem=ss.at[n], recv_sem=rs.at[n],
            device_id=dev, device_id_type=MESH,
        )

    def send(region, n, dev):
        cp = copy(region, n, dev)
        cp.start()
        sent.append(cp)

    def recv(region, n):
        copy(region, n, dp_of(x + 1, z)).wait_recv()

    ALL = slice(None)
    a_rows, b_rows = (0, A_ROWS), (A_ROWS, B_ROWS)

    def halves(rows, plus):
        return ((rows[0], plus), (rows[0] + plus, rows[1] - plus))

    a_half = halves(a_rows, A_PLUS)
    bz_half, bx_half = halves(b_rows, BZ_PLUS), halves(b_rows, BX_PLUS)

    def wreg(h, xx, zz, rows):
        return wall.at[h, xx, zz, pl.ds(*rows), :]

    SIGN = (1, -1)

    class Ring:
        def __init__(self, name, h, axis, rows, cut, wide):
            self.name, self.h, self.axis = name, h, axis
            self.rows, self.cut, self.wide = rows, cut, wide
            self.far = (NX if axis == "x" else NZ) // 2

        def dev(self, d):
            return dp_of(x + SIGN[d], z) if self.axis == "x" else dp_of(x, z + SIGN[d])

        def region(self, d, t):
            rows = self.cut[d] if t == self.far else self.rows
            if self.axis == "x":
                return wreg(self.h, wrap(x - SIGN[d] * t, NX), ALL if self.wide else z, rows)
            return wreg(self.h, ALL if self.wide else x, wrap(z - SIGN[d] * t, NZ), rows)

        def begin(self):
            for d in (0, 1):
                send(self.region(d, 0), W_ID[self.h, self.name, d, 1], self.dev(d))

        def step(self, t):
            for d in (0, 1):
                recv(self.region(d, t), W_ID[self.h, self.name, d, t])
                if t < self.far:
                    hop = self.region(d, t)
                    if t + 1 == self.far:
                        rows = self.cut[d]
                        if self.axis == "x":
                            hop = wreg(self.h, wrap(x - SIGN[d] * t, NX), ALL if self.wide else z, rows)
                        else:
                            hop = wreg(self.h, ALL if self.wide else x, wrap(z - SIGN[d] * t, NZ), rows)
                    send(hop, W_ID[self.h, self.name, d, t + 1], self.dev(d))

    AX = [Ring("ax", h, "x", a_rows, a_half, False) for h in range(HEADS)]
    BZ = [Ring("bz", h, "z", b_rows, bz_half, False) for h in range(HEADS)]
    AZ = [Ring("az", h, "z", a_rows, a_half, True) for h in range(HEADS)]
    BX = [Ring("bx", h, "x", b_rows, bx_half, True) for h in range(HEADS)]

    for h in range(HEADS):
        BZ[h].begin()
        AX[h].begin()

    kept = [keep[e : e + 1, :] >= 0 for e in range(KEEP)]
    mine = [keep[e : e + 1, :] - j_me * KEEP for e in range(KEEP)]
    slots = [slot[e : e + 1, :] for e in range(KEEP)]
    target = []
    for e in range(KEEP):
        rank = jnp.zeros((1, NDP), jnp.int32)
        for f in range(KEEP):
            if f != e:
                rank = rank + jnp.where(kept[f] & (slots[f] < slots[e]), 1, 0)
        target.append(row[e : e + 1, :] * KEEP + rank + 1)
    flat = jnp.zeros((8, BLK), F32)
    for t in range(KEEP):
        aim = jnp.zeros((1, NDP), jnp.int32)
        for e in range(KEEP):
            aim = aim + jnp.where(kept[e] & (mine[e] == t), target[e], 0)
        spread = one_hot(iota((NDP, BLK), 1) == iota((NDP, BLK), 0) * KEEP + t)
        aim = jnp.broadcast_to(aim.astype(F32), (8, NDP)).astype(BF16)
        flat = flat + jnp.dot(aim, spread, preferred_element_type=F32)
    flat = flat[0:1, :].astype(jnp.int32) - 1
    r_id = iota((512, BLK), 0)
    hit = ((r_id >> 4) * KEEP + (r_id & 3)) == flat
    pick = jnp.concatenate([one_hot(hit & (((r_id >> 2) & 3) == q)) for q in range(4)], axis=1)
    for n in range(4):
        cols = jnp.concatenate(
            [xn[:, q * 1024 + n * 256 : q * 1024 + (n + 1) * 256] for q in range(4)], axis=0
        )
        moved = jnp.dot(pick, cols, preferred_element_type=F32).astype(BF16)
        snd[:, :, n * 256 : (n + 1) * 256] = moved.reshape(NDP, 16, 256)

    ORDER = (0, 1, 3, 2)
    for dx in ORDER:
        if dx == 0:
            pltpu.make_async_copy(snd.at[p_me], rcv.at[p_me], a2a_r.at[x]).start()

        @pl.loop(1 if dx == 0 else 0, NZ)
        def _(dz):
            dev = dp_of(x + dx, z + dz)
            pltpu.make_async_remote_copy(
                src_ref=snd.at[dev["dp"]], dst_ref=rcv.at[p_me], send_sem=a2a_s,
                recv_sem=a2a_r.at[x], device_id=dev, device_id_type=MESH,
            ).start()

    s_id, l_id = iota((BLK, BLK), 0), iota((BLK, BLK), 1)
    lanes = l_id.astype(F32)
    for j in range(NT):
        across = seg[:, j * BLK : (j + 1) * BLK].astype(F32)
        down = jnp.sum(jnp.where(s_id == l_id, across, 0.0), axis=1, keepdims=True)
        rank = jnp.sum(jnp.where((down == across) & (l_id < s_id), 1.0, 0.0), axis=1, keepdims=True)
        aim = jnp.where(down >= 0, jnp.floor(down * (1.0 / 32.0)) * KEEP + rank, -1.0)
        hit = jnp.where(aim == lanes, 1.0, 0.0)
        place[j] = hit.astype(BF16)
        present[j : j + 1, :] = jnp.sum(hit, axis=0, keepdims=True)
    wide = iota((BLK, 8 * BLK), 1)
    spread = one_hot(iota((BLK, 8 * BLK), 0) == (wide >> 7) * 16 + (wide & 15))
    valid = jnp.dot(present[...].astype(BF16), spread, preferred_element_type=F32)
    pick_j = ((iota((NT, 8 * BLK), 1) & 127) >> 4) == iota((NT, 8 * BLK), 0)
    valid = jnp.sum(jnp.where(pick_j, valid, 0.0), axis=0, keepdims=True)
    same = ((s_id & 15) >> 2) == ((l_id & 15) >> 2)
    for pg in range(8):
        live = same & (valid[:, pg * BLK : (pg + 1) * BLK] > 0.5)
        bias[pg] = jnp.where(live, 0.0, -1e30)

    o_id, i_id = iota((BLK, BLK), 0), iota((BLK, BLK), 1)
    src = ((o_id & 31) >> 2) * 16 + (o_id >> 5) * 4 + (o_id & 3)
    unpick = one_hot(i_id == src)

    def nreg(j, g, half=None):
        if half is None:
            return nrm.at[j, pl.ds(pl.multiple_of(g * 32, 32), 32), :]
        return nrm.at[j, pl.ds(pl.multiple_of(g * 32 + half * 16, 16), 16), :]

    up, down_, twin = ten_of(y + 1, c), ten_of(y - 1, c), ten_of(y, 1 - c)

    def jdx(yy, cc):
        return wrap(yy, NY) * 2 + cc

    def y_unpack(dx):
        g = wrap(x - dx, NX)
        group = rcv.at[pl.ds(pl.multiple_of(g * NZ, NZ), NZ)]
        pltpu.make_async_copy(group, group, a2a_r.at[g]).wait()
        got = rcv[pl.ds(pl.multiple_of(g * NZ, NZ), NZ)].reshape(BLK, 1024)
        back = jnp.dot(unpick, got, preferred_element_type=F32).astype(BF16)
        at = pl.ds(pl.multiple_of(g * 32, 32), 32)
        for q in range(4):
            nrm[j_me, at, q * 1024 : (q + 1) * 1024] = back[q * 32 : (q + 1) * 32, :]
        own = nreg(j_me, g)
        send(own, Y_ID[dx, "p1"], up)
        send(own, Y_ID[dx, "m1"], down_)
        send(own, Y_ID[dx, "own"], twin)

    def y_near(dx):
        g = wrap(x - dx, NX)
        lo, hi = jdx(y - 1, c), jdx(y + 1, c)
        recv(nreg(lo, g), Y_ID[dx, "p1"])
        send(nreg(lo, g, 0), Y_ID[dx, "p2"], up)
        send(nreg(lo, g), Y_ID[dx, "fp1"], twin)
        recv(nreg(hi, g), Y_ID[dx, "m1"])
        send(nreg(hi, g, 1), Y_ID[dx, "m2"], down_)
        send(nreg(hi, g), Y_ID[dx, "fm1"], twin)

    def y_far(dx):
        g = wrap(x - dx, NX)
        far = jdx(y + 2, c)
        recv(nreg(far, g, 0), Y_ID[dx, "p2"])
        recv(nreg(far, g, 1), Y_ID[dx, "m2"])
        send(nreg(far, g), Y_ID[dx, "f2"], twin)

    def y_end(dx):
        g = wrap(x - dx, NX)
        recv(nreg(jdx(y, 1 - c), g), Y_ID[dx, "own"])
        recv(nreg(jdx(y - 1, 1 - c), g), Y_ID[dx, "fp1"])
        recv(nreg(jdx(y + 1, 1 - c), g), Y_ID[dx, "fm1"])
        recv(nreg(jdx(y + 2, 1 - c), g), Y_ID[dx, "f2"])

    def e(n, h):
        if n == 1:
            BZ[h].step(1)
            AX[h].step(1)
        elif n == 2:
            BZ[h].step(2)
            AX[h].step(2)
            AZ[h].begin()
        elif n == 3:
            BZ[h].step(3)
        else:
            BZ[h].step(4)
            BX[h].begin()

    def f(n, h):
        if n == 4:
            BX[h].step(1)
        elif n == 6:
            BX[h].step(2)
        else:
            AZ[h].step({1: 1, 2: 2, 3: 3, 5: 4}[n])

    def qkv_of(h):
        @pl.loop(0, NT // 2)
        def _(m):
            lhs = nrm[pl.ds(m * 2, 2)].reshape(2 * BLK, NDP * BLK)
            rhs = wall[h].reshape(NDP * BLK, 3 * HS)
            acc = jnp.dot(lhs, rhs, preferred_element_type=F32)
            col = iota(acc.shape, 1)
            acc = acc * jnp.where(col < HS, HS ** (-0.5), 1.0)
            qkv[pl.ds(m * 2, 2)] = acc.astype(BF16).reshape(2, BLK, 3 * HS)

    def attend(h):
        for pg in range(8):
            part = qkv[:, pg * 16 : (pg + 1) * 16, :].reshape(BLK, 3 * HS)
            q, k, v = part[:, :HS], part[:, HS : 2 * HS], part[:, 2 * HS :]
            s = lax.dot_general(q, k, (((1,), (1,)), ((), ())), preferred_element_type=F32)
            s = s + bias[pg]
            s = jnp.exp(s - jnp.max(s, axis=1, keepdims=True))
            w = (s / jnp.sum(s, axis=1, keepdims=True)).astype(BF16)
            o = jnp.dot(w, v, preferred_element_type=F32).astype(BF16)
            att[:, pg * 16 : (pg + 1) * 16, h * HS : (h + 1) * HS] = o.reshape(NT, 16, HS)

    e(1, 0)
    e(1, 1)
    e(2, 0)
    e(1, 2)
    e(2, 1)
    y_unpack(0)
    e(3, 0)
    e(2, 2)
    e(3, 1)
    e(4, 0)
    y_unpack(1)
    f(1, 0)
    e(3, 2)
    e(4, 1)
    y_near(0)
    f(2, 0)
    f(1, 1)
    e(4, 2)
    y_unpack(3)
    f(3, 0)
    f(2, 1)
    f(1, 2)
    y_far(0)
    y_near(1)
    f(4, 0)
    f(3, 1)
    f(2, 2)
    y_unpack(2)
    f(5, 0)
    f(3, 2)
    y_far(1)
    y_near(3)
    f(5, 1)
    f(4, 1)
    f(5, 2)
    y_far(3)
    y_near(2)
    y_far(2)
    f(6, 0)
    f(4, 2)
    for dx in ORDER:
        y_end(dx)
    f(6, 1)
    f(6, 2)

    for h in range(HEADS):
        qkv_of(h)
        attend(h)
    for j in range(NT):
        out[j * BLK : (j + 1) * BLK, :] = jnp.dot(
            place[j], att[j], preferred_element_type=F32
        ).astype(BF16)

    for cp in sent:
        cp.wait_send()
    most = snd.at[pl.ds(0, NDP - 1)]
    pltpu.make_async_copy(most, most, a2a_s).wait()


def body(tubelets, keep_index, dest_row, dest_slot, segment, ln_gain, w_query, w_key, w_value):
    width = tubelets.shape[2]
    vmem = pl.BlockSpec(memory_space=pltpu.VMEM)
    hbm = pl.BlockSpec(memory_space=pl.ANY)
    dma = pltpu.SemaphoreType.DMA
    cols = w_query.shape[1]
    mixed = pl.pallas_call(
        kernel,
        out_shape=jax.ShapeDtypeStruct((NT * BLK, cols), BF16),
        in_specs=[vmem] * 6 + [hbm] * 3,
        out_specs=vmem,
        scratch_shapes=[
            pltpu.VMEM((BLK, width), BF16),
            pltpu.VMEM((NDP, 16, width // 4), BF16),
            pltpu.VMEM((NDP, 16, width // 4), BF16),
            pltpu.VMEM((NT, BLK, width), BF16),
            pltpu.VMEM((HEADS, NX, NZ, BLK, 3 * HS), BF16),
            pltpu.VMEM((NT, BLK, 3 * HS), BF16),
            pltpu.VMEM((NT, BLK, cols), BF16),
            pltpu.VMEM((8, BLK, BLK), F32),
            pltpu.VMEM((NT, BLK, BLK), BF16),
            pltpu.VMEM((NT, BLK), F32),
            dma((3 * HEADS,)),
            dma,
            dma((NX,)),
            dma((N_MSG,)),
            dma((N_MSG,)),
        ],
        compiler_params=pltpu.CompilerParams(
            collective_id=0, has_side_effects=True, vmem_limit_bytes=60 * 1024 * 1024
        ),
        name="repack_attend",
    )(
        tubelets.reshape(BLK, width),
        keep_index.T,
        dest_row.T,
        dest_slot.T,
        segment,
        ln_gain.reshape(1, width),
        w_query,
        w_key,
        w_value,
    )
    return mixed.reshape(1, NT * BLK, cols)


def solution(mesh):
    return jax.shard_map(
        body,
        mesh=mesh,
        in_specs=(
            P("dp", "tensor", None),
            P("dp", "tensor"),
            P("dp", "tensor"),
            P("dp", "tensor"),
            P("dp", None),
            P(),
            P("dp", "tensor"),
            P("dp", "tensor"),
            P("dp", "tensor"),
        ),
        out_specs=P("dp", None, "tensor"),
        check_vma=False,
    )
```

time: 344 us -> 135 us (0.39)
  waiting for transfers between devices: 251 us -> 0 us
  Pallas kernels: 0 us -> 129 us
  matrix products: 43.3 us -> 0 us
  starting transfers between devices: 15.6 us -> 0 us
  between operations: 13.4 us -> 0.01 us
  other arithmetic: 7.78 us -> 0 us
  local copies, waits for them, and re-layouts: 12.3 us -> 5.56 us
    all_gather x4 -> x0, waiting for transfers between devices: 216 us -> none  [the longest x1 74 us: body(): lax.all_gather(w_key, 'dp', axis=0, tiled=True)]
    pallas_call x0 -> x1, Pallas kernels: none -> 129 us  [body(): pl.pallas_call(kernel, out_shape=jax.ShapeDtypeStruct((NT * BLK, cols), B...]
    all_to_all x2 -> x0, waiting for transfers between devices: 33.9 us -> none  [the longest x1 28.2 us: body(): lax.all_to_all(send_rows, 'dp', split_axis=0, concat_axis=0, tiled=True)]
    dot_general x5 -> x0, matrix products: 32.4 us -> none  [the longest x3 24.2 us: body(): jnp.dot(normed_row, piece_w, preferred_element_type=jnp.float32)]
    all_to_all x2 -> x0, starting transfers between devices: 15.4 us -> none  [the longest x1 11.3 us: body(): lax.all_to_all(send_slots, 'dp', split_axis=0, concat_axis=0, tiled=True)]
    sub x2 -> x0, matrix products: 10.8 us -> none  [attend(): weights = jnp.where(allowed[None], jnp.exp(masked - largest), 0.0)]
  transfers between devices with their start and end apart: 6 -> 0, of which waited for: 6 -> 0; matrix products, arithmetic and copies ran while one was open for 9% -> 0% of each run, Pallas kernels for 0% -> 0%
where the time goes in v1:
time: 135 us; the launch traced here: 134 us
  Pallas kernels  129 us (96%)
  local copies, waits for them, and re-layouts  5.56 us (4%)
    pallas_call x1, Pallas kernels, body(): pl.pallas_call(kernel, out_shape=jax.ShapeDtypeStruct((NT * BLK, cols), B...  129 us

profile of v1, /device:TPU:16, one launch (start us, length us, event | category | flops | bytes accessed | tf_op | source)
XLA Modules:
  0.0 134.4 jit_solution(883568254281541003)
XLA Ops:
  0.0 1.3 reshape.10.gain
  1.3 2.2 %reshape.9.tub = bf16[128,4096]{1,0:T(8,128)(2,1)} reshape(bf16[32,4,4096]{2,1,0:T(4,128)(2,1)} %param.9) | data formatting | bytes 2097152 | tf_op jit(solution)/shard_map/reshape | solution.py:414
  3.5 128.8 %repack_attend.1 = bf16[1024,384]{1,0:T(8,128)(2,1)} custom-call(bf16[128,4096]{1,0:T(8,128)(2,1)} %reshape.9.tub, s32[4,32]{1,0:T(4,128)} %bitcast.5, s32[4,32]{1,0:T(4,128)} %bitcast.6, s32[4,32]{1,0:T(4,128)} %bitcast.7, s32[1,1024]{1,0:T(1,128)} %seg.1, bf16[1,4096]{1,0:T(2,128)(2,1)} %reshape.10.gain, bf16[128,384]{1,0:T(8,128)(2,1)} %wq.1, ...), custom_call_target="tpu_custom_call" | custom-call | tf_op jit(solution)/shard_map/repack_attend/pallas_call | solution.py:387
  132.3 2.1 %copy.11 = bf16[1,1024,384]{2,1,0:T(8,128)(2,1)} copy(bf16[1,1024,384]{2,1,0:T(8,128)(2,1)} %bitcast.4) | data formatting | bytes 1572864

commit v2 on v1

--- a/solution.py
+++ b/solution.py
@@ -15,21 +15,45 @@
 HEADS = 3
 BLK = 128
 
-A_ROWS, A_PLUS = 48, 16
+A_ROWS, A_PLUS = 32, 16
 B_ROWS = BLK - A_ROWS
-BZ_PLUS, BX_PLUS = 32, 32
+BZ_PLUS, BX_PLUS = 48, 48
+
+SHIFTS = (0, 1, -1, 2, -2, 3, -3, 4)
 
 W_KEYS = (
     [("ax", d, t) for t in (1, 2) for d in (0, 1)]
     + [("bz", d, t) for t in (1, 2, 3, 4) for d in (0, 1)]
     + [("az", d, t) for t in (1, 2, 3, 4) for d in (0, 1)]
-    + [("bx", d, t) for t in (1, 2) for d in (0, 1)]
+    + [(("bx", s), d, t) for s in SHIFTS for t in (1, 2) for d in (0, 1)]
 )
 W_ID = {(h,) + key: h * len(W_KEYS) + n for h in range(HEADS) for n, key in enumerate(W_KEYS)}
 Y_KEYS = ("p1", "m1", "p2", "m2", "own", "fp1", "fm1", "f2")
 Y_ID = {(g, key): len(W_ID) + g * len(Y_KEYS) + n for g in range(NX) for n, key in enumerate(Y_KEYS)}
 N_MSG = len(W_ID) + len(Y_ID)
 
+PLAN = (
+    ("ax", 0, 1), ("bz", 0, 1), ("bx", 0, 0, 1), ("ax", 1, 1), ("bz", 1, 1), ("bx", 1, 0, 1), ("ax", 0, 2),
+    ("bx", 0, 1, 1), ("bx", 0, -1, 1), ("bx", 0, 0, 2), ("ax", 1, 2), ("yu", 0), ("A", 3), ("A", 2),
+    ("bx", 1, 1, 1), ("bz", 0, 2), ("bx", 1, -1, 1), ("bx", 1, 0, 2), ("bx", 0, 1, 2), ("yu", 1), ("bz", 1, 2),
+    ("bx", 0, -1, 2), ("az", 0, 1), ("yn", 0), ("pl",), ("yn", 1), ("bx", 1, 1, 2), ("bx", 0, 2, 1), ("yf", 0),
+    ("yu", 3), ("bx", 0, -2, 1), ("bx", 1, -1, 2), ("ye", 0), ("bx", 1, 2, 1), ("yf", 1), ("az", 1, 1),
+    ("bx", 1, -2, 1), ("bx", 0, 2, 2), ("ye", 1), ("bx", 0, -2, 2), ("bz", 0, 3), ("bx", 1, 2, 2),
+    ("bx", 1, -2, 2), ("yu", 2), ("bz", 1, 3), ("yn", 3), ("bx", 0, 3, 1), ("az", 0, 2), ("bx", 0, -3, 1),
+    ("bx", 1, 3, 1), ("az", 1, 2), ("bz", 0, 4), ("W", 2), ("bx", 1, -3, 1), ("bz", 1, 4), ("bx", 0, 3, 2),
+    ("yn", 2), ("bx", 0, -3, 2), ("bx", 1, 3, 2), ("az", 0, 3), ("bx", 0, 4, 1), ("yf", 3), ("ax", 2, 1),
+    ("az", 1, 3), ("bx", 2, 0, 1), ("bz", 2, 1), ("ye", 3), ("bx", 1, -3, 2), ("yf", 2), ("az", 0, 4),
+    ("bx", 1, 4, 1), ("az", 1, 4), ("bx", 0, 4, 2), ("ax", 2, 2), ("ye", 2), ("q", 0, 0), ("bx", 2, 0, 2),
+    ("bz", 2, 2), ("bx", 2, 1, 1), ("q", 0, 1), ("az", 2, 1), ("bx", 2, -1, 1), ("bx", 1, 4, 2),
+    ("bx", 2, 2, 1), ("bz", 2, 3), ("t", 0), ("bx", 2, -2, 1), ("bx", 2, 1, 2), ("q", 1, 0), ("bx", 2, -1, 2),
+    ("az", 2, 2), ("bx", 2, 2, 2), ("bz", 2, 4), ("bx", 2, 3, 1), ("q", 1, 1), ("bx", 2, -3, 1),
+    ("bx", 2, -2, 2), ("t", 1), ("bx", 2, 4, 1), ("az", 2, 3), ("bx", 2, 3, 2), ("bx", 2, -3, 2),
+    ("bx", 2, 4, 2), ("az", 2, 4), ("q", 2, 0), ("q", 2, 1), ("t", 2),
+)
+
+
+FIRST_GROUPS, FIRST_HEADS = (0, 1), (0, 1)
+
 
 def iota(shape, dim):
     return lax.broadcasted_iota(jnp.int32, shape, dim)
@@ -40,10 +64,11 @@
 
 
 def kernel(
-    tub, keep, row, slot, seg, gain, wq, wk, wv, out,
-    xn, snd, rcv, nrm, wall, qkv, att, bias, place, present,
-    lsem, a2a_s, a2a_r, ss, rs,
+    tub_hbm, keep, row, slot, seg, gain, wq, wk, wv, out,
+    tub, gains, xn, snd, rcv, nrm, wall, qkv, att, bias, place, present,
+    lsem, a2a_s, a2a_r, ss, rs, entered,
 ):
+    width = xn.shape[1]
     p_me, j_me = lax.axis_index("dp"), lax.axis_index("tensor")
     x, z = p_me // NZ, lax.rem(p_me, NZ)
     y, c = j_me // 2, lax.rem(j_me, 2)
@@ -58,15 +83,14 @@
         return {"tensor": wrap(yy, NY) * 2 + cc}
 
     barrier = pltpu.get_barrier_semaphore()
-
-    @pl.loop(1, NDP)
-    def _(d):
-        pl.semaphore_signal(
-            barrier, inc=1, device_id={"dp": lax.rem(p_me + d, NDP)}, device_id_type=MESH
-        )
-
-    for dev in (ten_of(y + 1, c), ten_of(y - 1, c), ten_of(y, 1 - c)):
+    near = [dp_of(x + d, z) for d in range(1, NX)]
+    peers = near + [dp_of(x, z + d) for d in range(1, NZ)]
+    peers += [ten_of(y + 1, c), ten_of(y - 1, c), ten_of(y, 1 - c)]
+    for dev in peers:
         pl.semaphore_signal(barrier, inc=1, device_id=dev, device_id_type=MESH)
+
+    load = pltpu.make_async_copy(tub_hbm, tub, lsem.at[3 * HEADS])
+    load.start()
 
     local = []
     for h in range(HEADS):
@@ -79,15 +103,19 @@
             cp.start()
             local.append(cp)
 
-    @pl.loop(0, BLK // 16)
-    def _(i):
-        at = pl.ds(pl.multiple_of(i * 16, 16), 16)
-        v = tub[at, :].astype(F32)
+    for n in range(width // BLK):
+        gains[:, n * BLK : (n + 1) * BLK] = jnp.broadcast_to(gain[n : n + 1, :].astype(F32), (8, BLK))
+
+    load.wait()
+    for t in range(KEEP):
+        v = tub[:, t, :].astype(F32)
         v = v - jnp.mean(v, axis=-1, keepdims=True)
         var = jnp.mean(v * v, axis=-1, keepdims=True)
-        xn[at, :] = (v * lax.rsqrt(var + 1e-06) * gain[...].astype(F32)).astype(BF16)
-
-    pl.semaphore_wait(barrier, NDP - 1 + 3)
+        xn[t * NDP : (t + 1) * NDP, :] = (v * lax.rsqrt(var + 1e-06) * gains[0:1, :]).astype(BF16)
+
+    pl.semaphore_wait(barrier, len(peers))
+    for dev in near:
+        pl.semaphore_signal(entered, inc=1, device_id=dev, device_id_type=MESH)
     for cp in local:
         cp.wait()
 
@@ -122,9 +150,9 @@
     SIGN = (1, -1)
 
     class Ring:
-        def __init__(self, name, h, axis, rows, cut, wide):
+        def __init__(self, name, h, axis, rows, cut, wide, zz=z):
             self.name, self.h, self.axis = name, h, axis
-            self.rows, self.cut, self.wide = rows, cut, wide
+            self.rows, self.cut, self.wide, self.zz = rows, cut, wide, zz
             self.far = (NX if axis == "x" else NZ) // 2
 
         def dev(self, d):
@@ -133,7 +161,7 @@
         def region(self, d, t):
             rows = self.cut[d] if t == self.far else self.rows
             if self.axis == "x":
-                return wreg(self.h, wrap(x - SIGN[d] * t, NX), ALL if self.wide else z, rows)
+                return wreg(self.h, wrap(x - SIGN[d] * t, NX), self.zz, rows)
             return wreg(self.h, ALL if self.wide else x, wrap(z - SIGN[d] * t, NZ), rows)
 
         def begin(self):
@@ -148,7 +176,7 @@
                     if t + 1 == self.far:
                         rows = self.cut[d]
                         if self.axis == "x":
-                            hop = wreg(self.h, wrap(x - SIGN[d] * t, NX), ALL if self.wide else z, rows)
+                            hop = wreg(self.h, wrap(x - SIGN[d] * t, NX), self.zz, rows)
                         else:
                             hop = wreg(self.h, ALL if self.wide else x, wrap(z - SIGN[d] * t, NZ), rows)
                     send(hop, W_ID[self.h, self.name, d, t + 1], self.dev(d))
@@ -156,11 +184,18 @@
     AX = [Ring("ax", h, "x", a_rows, a_half, False) for h in range(HEADS)]
     BZ = [Ring("bz", h, "z", b_rows, bz_half, False) for h in range(HEADS)]
     AZ = [Ring("az", h, "z", a_rows, a_half, True) for h in range(HEADS)]
-    BX = [Ring("bx", h, "x", b_rows, bx_half, True) for h in range(HEADS)]
-
-    for h in range(HEADS):
+    BX = [
+        {s: Ring(("bx", s), h, "x", b_rows, bx_half, False, wrap(z - s, NZ)) for s in SHIFTS}
+        for h in range(HEADS)
+    ]
+
+    def begin(h):
         BZ[h].begin()
         AX[h].begin()
+        BX[h][0].begin()
+
+    for h in FIRST_HEADS:
+        begin(h)
 
     kept = [keep[e : e + 1, :] >= 0 for e in range(KEEP)]
     mine = [keep[e : e + 1, :] - j_me * KEEP for e in range(KEEP)]
@@ -172,15 +207,13 @@
             if f != e:
                 rank = rank + jnp.where(kept[f] & (slots[f] < slots[e]), 1, 0)
         target.append(row[e : e + 1, :] * KEEP + rank + 1)
-    flat = jnp.zeros((8, BLK), F32)
+    aims = []
     for t in range(KEEP):
         aim = jnp.zeros((1, NDP), jnp.int32)
         for e in range(KEEP):
             aim = aim + jnp.where(kept[e] & (mine[e] == t), target[e], 0)
-        spread = one_hot(iota((NDP, BLK), 1) == iota((NDP, BLK), 0) * KEEP + t)
-        aim = jnp.broadcast_to(aim.astype(F32), (8, NDP)).astype(BF16)
-        flat = flat + jnp.dot(aim, spread, preferred_element_type=F32)
-    flat = flat[0:1, :].astype(jnp.int32) - 1
+        aims.append(aim)
+    flat = jnp.concatenate(aims, axis=1) - 1
     r_id = iota((512, BLK), 0)
     hit = ((r_id >> 4) * KEEP + (r_id & 3)) == flat
     pick = jnp.concatenate([one_hot(hit & (((r_id >> 2) & 3) == q)) for q in range(4)], axis=1)
@@ -191,8 +224,9 @@
         moved = jnp.dot(pick, cols, preferred_element_type=F32).astype(BF16)
         snd[:, :, n * 256 : (n + 1) * 256] = moved.reshape(NDP, 16, 256)
 
-    ORDER = (0, 1, 3, 2)
-    for dx in ORDER:
+    pl.semaphore_wait(entered, len(near))
+
+    def exchange(dx):
         if dx == 0:
             pltpu.make_async_copy(snd.at[p_me], rcv.at[p_me], a2a_r.at[x]).start()
 
@@ -204,25 +238,30 @@
                 recv_sem=a2a_r.at[x], device_id=dev, device_id_type=MESH,
             ).start()
 
+    for dx in FIRST_GROUPS:
+        exchange(dx)
+
     s_id, l_id = iota((BLK, BLK), 0), iota((BLK, BLK), 1)
     lanes = l_id.astype(F32)
-    for j in range(NT):
-        across = seg[:, j * BLK : (j + 1) * BLK].astype(F32)
-        down = jnp.sum(jnp.where(s_id == l_id, across, 0.0), axis=1, keepdims=True)
-        rank = jnp.sum(jnp.where((down == across) & (l_id < s_id), 1.0, 0.0), axis=1, keepdims=True)
-        aim = jnp.where(down >= 0, jnp.floor(down * (1.0 / 32.0)) * KEEP + rank, -1.0)
-        hit = jnp.where(aim == lanes, 1.0, 0.0)
-        place[j] = hit.astype(BF16)
-        present[j : j + 1, :] = jnp.sum(hit, axis=0, keepdims=True)
-    wide = iota((BLK, 8 * BLK), 1)
-    spread = one_hot(iota((BLK, 8 * BLK), 0) == (wide >> 7) * 16 + (wide & 15))
-    valid = jnp.dot(present[...].astype(BF16), spread, preferred_element_type=F32)
-    pick_j = ((iota((NT, 8 * BLK), 1) & 127) >> 4) == iota((NT, 8 * BLK), 0)
-    valid = jnp.sum(jnp.where(pick_j, valid, 0.0), axis=0, keepdims=True)
-    same = ((s_id & 15) >> 2) == ((l_id & 15) >> 2)
-    for pg in range(8):
-        live = same & (valid[:, pg * BLK : (pg + 1) * BLK] > 0.5)
-        bias[pg] = jnp.where(live, 0.0, -1e30)
+
+    def slot_order():
+        for j in range(NT):
+            across = seg[:, j * BLK : (j + 1) * BLK].astype(F32)
+            down = jnp.sum(jnp.where(s_id == l_id, across, 0.0), axis=1, keepdims=True)
+            rank = jnp.sum(jnp.where((down == across) & (l_id < s_id), 1.0, 0.0), axis=1, keepdims=True)
+            aim = jnp.where(down >= 0, jnp.floor(down * (1.0 / 32.0)) * KEEP + rank, -1.0)
+            hit = jnp.where(aim == lanes, 1.0, 0.0)
+            place[j] = hit.astype(BF16)
+            present[j : j + 1, :] = jnp.sum(hit, axis=0, keepdims=True)
+        wide = iota((BLK, 8 * BLK), 1)
+        spread = one_hot(iota((BLK, 8 * BLK), 0) == (wide >> 7) * 16 + (wide & 15))
+        valid = jnp.dot(present[...].astype(BF16), spread, preferred_element_type=F32)
+        pick_j = ((iota((NT, 8 * BLK), 1) & 127) >> 4) == iota((NT, 8 * BLK), 0)
+        valid = jnp.sum(jnp.where(pick_j, valid, 0.0), axis=0, keepdims=True)
+        same = ((s_id & 15) >> 2) == ((l_id & 15) >> 2)
+        for pg in range(8):
+            live = same & (valid[:, pg * BLK : (pg + 1) * BLK] > 0.5)
+            bias[pg] = jnp.where(live, 0.0, -1e30)
 
     o_id, i_id = iota((BLK, BLK), 0), iota((BLK, BLK), 1)
     src = ((o_id & 31) >> 2) * 16 + (o_id >> 5) * 4 + (o_id & 3)
@@ -276,30 +315,20 @@
         recv(nreg(jdx(y + 1, 1 - c), g), Y_ID[dx, "fm1"])
         recv(nreg(jdx(y + 2, 1 - c), g), Y_ID[dx, "f2"])
 
-    def e(n, h):
-        if n == 1:
-            BZ[h].step(1)
-            AX[h].step(1)
-        elif n == 2:
-            BZ[h].step(2)
-            AX[h].step(2)
+    def weights(name, h, *at):
+        if name == "bx":
+            BX[h][at[0]].step(at[1])
+            return
+        t = at[0]
+        {"ax": AX, "bz": BZ, "az": AZ}[name][h].step(t)
+        if name == "ax" and t == 2:
             AZ[h].begin()
-        elif n == 3:
-            BZ[h].step(3)
-        else:
-            BZ[h].step(4)
-            BX[h].begin()
-
-    def f(n, h):
-        if n == 4:
-            BX[h].step(1)
-        elif n == 6:
-            BX[h].step(2)
-        else:
-            AZ[h].step({1: 1, 2: 2, 3: 3, 5: 4}[n])
-
-    def qkv_of(h):
-        @pl.loop(0, NT // 2)
+        if name == "bz":
+            for s in (t, -t) if t < 4 else (t,):
+                BX[h][s].begin()
+
+    def qkv_of(h, half):
+        @pl.loop(half * 2, half * 2 + 2)
         def _(m):
             lhs = nrm[pl.ds(m * 2, 2)].reshape(2 * BLK, NDP * BLK)
             rhs = wall[h].reshape(NDP * BLK, 3 * HS)
@@ -319,54 +348,16 @@
             o = jnp.dot(w, v, preferred_element_type=F32).astype(BF16)
             att[:, pg * 16 : (pg + 1) * 16, h * HS : (h + 1) * HS] = o.reshape(NT, 16, HS)
 
-    e(1, 0)
-    e(1, 1)
-    e(2, 0)
-    e(1, 2)
-    e(2, 1)
-    y_unpack(0)
-    e(3, 0)
-    e(2, 2)
-    e(3, 1)
-    e(4, 0)
-    y_unpack(1)
-    f(1, 0)
-    e(3, 2)
-    e(4, 1)
-    y_near(0)
-    f(2, 0)
-    f(1, 1)
-    e(4, 2)
-    y_unpack(3)
-    f(3, 0)
-    f(2, 1)
-    f(1, 2)
-    y_far(0)
-    y_near(1)
-    f(4, 0)
-    f(3, 1)
-    f(2, 2)
-    y_unpack(2)
-    f(5, 0)
-    f(3, 2)
-    y_far(1)
-    y_near(3)
-    f(5, 1)
-    f(4, 1)
-    f(5, 2)
-    y_far(3)
-    y_near(2)
-    y_far(2)
-    f(6, 0)
-    f(4, 2)
-    for dx in ORDER:
-        y_end(dx)
-    f(6, 1)
-    f(6, 2)
-
-    for h in range(HEADS):
-        qkv_of(h)
-        attend(h)
+    acts = {
+        "yu": y_unpack, "yn": y_near, "yf": y_far, "ye": y_end, "A": exchange, "W": begin,
+        "pl": slot_order, "q": qkv_of, "t": attend,
+    }
+    for name, *rest in PLAN:
+        if name in acts:
+            acts[name](*rest)
+        else:
+            weights(name, *rest)
+
     for j in range(NT):
         out[j * BLK : (j + 1) * BLK, :] = jnp.dot(
             place[j], att[j], preferred_element_type=F32
@@ -387,9 +378,11 @@
     mixed = pl.pallas_call(
         kernel,
         out_shape=jax.ShapeDtypeStruct((NT * BLK, cols), BF16),
-        in_specs=[vmem] * 6 + [hbm] * 3,
+        in_specs=[hbm] + [vmem] * 5 + [hbm] * 3,
         out_specs=vmem,
         scratch_shapes=[
+            pltpu.VMEM(tubelets.shape, BF16),
+            pltpu.VMEM((8, width), F32),
             pltpu.VMEM((BLK, width), BF16),
             pltpu.VMEM((NDP, 16, width // 4), BF16),
             pltpu.VMEM((NDP, 16, width // 4), BF16),
@@ -400,23 +393,24 @@
             pltpu.VMEM((8, BLK, BLK), F32),
             pltpu.VMEM((NT, BLK, BLK), BF16),
             pltpu.VMEM((NT, BLK), F32),
-            dma((3 * HEADS,)),
+            dma((3 * HEADS + 1,)),
             dma,
             dma((NX,)),
             dma((N_MSG,)),
             dma((N_MSG,)),
+            pltpu.SemaphoreType.REGULAR,
         ],
         compiler_params=pltpu.CompilerParams(
             collective_id=0, has_side_effects=True, vmem_limit_bytes=60 * 1024 * 1024
         ),
         name="repack_attend",
     )(
-        tubelets.reshape(BLK, width),
+        tubelets,
         keep_index.T,
         dest_row.T,
         dest_slot.T,
         segment,
-        ln_gain.reshape(1, width),
+        ln_gain.reshape(width // BLK, BLK),
         w_query,
         w_key,
         w_value,

time: 135 us -> 104 us (0.77)
  Pallas kernels: 129 us -> 102 us
  local copies, waits for them, and re-layouts: 5.56 us -> 2.09 us
    pallas_call x1, Pallas kernels: 129 us -> 102 us  [body(): pl.pallas_call(kernel, out_shape=jax.ShapeDtypeStruct((NT * BLK, cols), B...]
    reshape x2 -> x0, local copies, waits for them, and re-layouts: 3.46 us -> none  [the longest x1 2.15 us: body(): tubelets.reshape(BLK, width)]
where the time goes in v2:
time: 104 us
  Pallas kernels  102 us (98%)
  local copies, waits for them, and re-layouts  2.09 us (2%)
    pallas_call x1, Pallas kernels, body(): pl.pallas_call(kernel, out_shape=jax.ShapeDtypeStruct((NT * BLK, cols), B...  102 us
    unnamed x1, local copies, waits for them, and re-layouts  2.09 us

profile of v2, /device:TPU:16, one launch (start us, length us, event | category | flops | bytes accessed | tf_op | source)
XLA Modules:
  0.0 103.9 jit_solution(6508475015341816879)
XLA Ops:
  0.0 101.8 %repack_attend.1 = bf16[1024,384]{1,0:T(8,128)(2,1)} custom-call(bf16[32,4,4096]{2,1,0:T(4,128)(2,1)} %tub_hbm.1, s32[4,32]{1,0:T(4,128)} %bitcast.7, s32[4,32]{1,0:T(4,128)} %bitcast.8, s32[4,32]{1,0:T(4,128)} %bitcast.9, s32[1,1024]{1,0:T(1,128)} %seg.1, bf16[32,128]{1,0:T(8,128)(2,1)} %bitcast.6, bf16[128,384]{1,0:T(8,128)(2,1)} %wq.1, ...), custom_call_target="tpu_custom_call" | custom-call | tf_op jit(solution)/shard_map/repack_attend/pallas_call | solution.py:378
  101.8 2.1 %copy.11 = bf16[1,1024,384]{2,1,0:T(8,128)(2,1)} copy(bf16[1,1024,384]{2,1,0:T(8,128)(2,1)} %bitcast.5) | data formatting | bytes 1572864

commit v3 on v2

--- a/solution.py
+++ b/solution.py
@@ -33,26 +33,26 @@
 N_MSG = len(W_ID) + len(Y_ID)
 
 PLAN = (
-    ("ax", 0, 1), ("bz", 0, 1), ("bx", 0, 0, 1), ("ax", 1, 1), ("bz", 1, 1), ("bx", 1, 0, 1), ("ax", 0, 2),
-    ("bx", 0, 1, 1), ("bx", 0, -1, 1), ("bx", 0, 0, 2), ("ax", 1, 2), ("yu", 0), ("A", 3), ("A", 2),
-    ("bx", 1, 1, 1), ("bz", 0, 2), ("bx", 1, -1, 1), ("bx", 1, 0, 2), ("bx", 0, 1, 2), ("yu", 1), ("bz", 1, 2),
-    ("bx", 0, -1, 2), ("az", 0, 1), ("yn", 0), ("pl",), ("yn", 1), ("bx", 1, 1, 2), ("bx", 0, 2, 1), ("yf", 0),
-    ("yu", 3), ("bx", 0, -2, 1), ("bx", 1, -1, 2), ("ye", 0), ("bx", 1, 2, 1), ("yf", 1), ("az", 1, 1),
-    ("bx", 1, -2, 1), ("bx", 0, 2, 2), ("ye", 1), ("bx", 0, -2, 2), ("bz", 0, 3), ("bx", 1, 2, 2),
-    ("bx", 1, -2, 2), ("yu", 2), ("bz", 1, 3), ("yn", 3), ("bx", 0, 3, 1), ("az", 0, 2), ("bx", 0, -3, 1),
-    ("bx", 1, 3, 1), ("az", 1, 2), ("bz", 0, 4), ("W", 2), ("bx", 1, -3, 1), ("bz", 1, 4), ("bx", 0, 3, 2),
-    ("yn", 2), ("bx", 0, -3, 2), ("bx", 1, 3, 2), ("az", 0, 3), ("bx", 0, 4, 1), ("yf", 3), ("ax", 2, 1),
-    ("az", 1, 3), ("bx", 2, 0, 1), ("bz", 2, 1), ("ye", 3), ("bx", 1, -3, 2), ("yf", 2), ("az", 0, 4),
-    ("bx", 1, 4, 1), ("az", 1, 4), ("bx", 0, 4, 2), ("ax", 2, 2), ("ye", 2), ("q", 0, 0), ("bx", 2, 0, 2),
-    ("bz", 2, 2), ("bx", 2, 1, 1), ("q", 0, 1), ("az", 2, 1), ("bx", 2, -1, 1), ("bx", 1, 4, 2),
-    ("bx", 2, 2, 1), ("bz", 2, 3), ("t", 0), ("bx", 2, -2, 1), ("bx", 2, 1, 2), ("q", 1, 0), ("bx", 2, -1, 2),
-    ("az", 2, 2), ("bx", 2, 2, 2), ("bz", 2, 4), ("bx", 2, 3, 1), ("q", 1, 1), ("bx", 2, -3, 1),
-    ("bx", 2, -2, 2), ("t", 1), ("bx", 2, 4, 1), ("az", 2, 3), ("bx", 2, 3, 2), ("bx", 2, -3, 2),
-    ("bx", 2, 4, 2), ("az", 2, 4), ("q", 2, 0), ("q", 2, 1), ("t", 2),
+    ("ax", 0, 1), ("bz", 0, 1), ("A", 1), ("bx", 0, 0, 1), ("ax", 1, 1), ("bz", 1, 1), ("bx", 1, 0, 1),
+    ("ax", 0, 2), ("bx", 0, 1, 1), ("bx", 0, -1, 1), ("bz", 0, 2), ("A", 3), ("bx", 0, 0, 2), ("ax", 1, 2),
+    ("yu", 0), ("A", 2), ("bx", 1, 1, 1), ("bx", 1, -1, 1), ("y0", 0), ("bx", 1, 0, 2), ("bz", 1, 2),
+    ("bx", 0, 1, 2), ("bx", 0, -1, 2), ("bx", 0, 2, 1), ("az", 0, 1), ("yn", 0), ("pl",), ("bx", 0, -2, 1),
+    ("yu", 1), ("bz", 0, 3), ("y1", 0), ("y0", 1), ("yf", 0), ("bx", 1, 1, 2), ("y2", 0), ("bx", 1, -1, 2),
+    ("bx", 1, 2, 1), ("yn", 1), ("yu", 3), ("bx", 1, -2, 1), ("bx", 0, 2, 2), ("bx", 0, -2, 2), ("y1", 1),
+    ("bx", 0, 3, 1), ("az", 1, 1), ("y0", 3), ("yf", 1), ("bx", 0, -3, 1), ("bx", 1, 2, 2), ("bz", 1, 3),
+    ("bx", 1, -2, 2), ("y2", 1), ("bx", 0, 3, 2), ("bx", 0, -3, 2), ("yu", 2), ("az", 0, 2), ("bz", 0, 4),
+    ("W", 2), ("bx", 1, 3, 1), ("yn", 3), ("y0", 2), ("bx", 1, -3, 1), ("az", 1, 2), ("bz", 1, 4),
+    ("bx", 0, 4, 1), ("ax", 2, 1), ("y1", 3), ("bx", 2, 0, 1), ("az", 0, 3), ("bx", 1, 3, 2), ("yn", 2),
+    ("bx", 1, -3, 2), ("bz", 2, 1), ("bx", 1, 4, 1), ("bx", 0, 4, 2), ("az", 1, 3), ("ax", 2, 2), ("yf", 3),
+    ("y1", 2), ("bx", 2, 0, 2), ("az", 0, 4), ("q", 0, 0, 0), ("q", 0, 0, 1), ("bx", 2, 1, 1), ("y2", 3),
+    ("bz", 2, 2), ("yf", 2), ("q", 0, 0, 2), ("bx", 2, -1, 1), ("az", 1, 4), ("q", 1, 0, 0), ("bx", 1, 4, 2),
+    ("bx", 2, 1, 2), ("y2", 2), ("q", 0, 0, 3), ("az", 2, 1), ("q", 0, 1), ("bx", 2, 2, 1), ("bz", 2, 3),
+    ("bx", 2, -2, 1), ("t", 0), ("bx", 2, -1, 2), ("q", 1, 0, 1), ("az", 2, 2), ("bx", 2, 2, 2),
+    ("q", 1, 0, 2), ("bz", 2, 4), ("q", 1, 0, 3), ("bx", 2, 3, 1), ("q", 1, 1), ("bx", 2, -3, 1), ("az", 2, 3),
+    ("bx", 2, -2, 2), ("t", 1), ("bx", 2, 4, 1), ("bx", 2, 3, 2), ("az", 2, 4), ("q", 2, 0, 0),
+    ("bx", 2, -3, 2), ("bx", 2, 4, 2), ("q", 2, 0, 1), ("q", 2, 0, 2), ("q", 2, 0, 3), ("q", 2, 1), ("t", 2),
 )
-
-
-FIRST_GROUPS, FIRST_HEADS = (0, 1), (0, 1)
+FIRST_GROUPS, FIRST_HEADS = (0,), (0, 1)
 
 
 def iota(shape, dim):
@@ -65,7 +65,7 @@
 
 def kernel(
     tub_hbm, keep, row, slot, seg, gain, wq, wk, wv, out,
-    tub, gains, xn, snd, rcv, nrm, wall, qkv, att, bias, place, present,
+    tub, gains, xn, snd, rcv, nrm, wall, acc, qkv, att, score, prob, bias, place, present,
     lsem, a2a_s, a2a_r, ss, rs, entered,
 ):
     width = xn.shape[1]
@@ -102,16 +102,6 @@
             )
             cp.start()
             local.append(cp)
-
-    for n in range(width // BLK):
-        gains[:, n * BLK : (n + 1) * BLK] = jnp.broadcast_to(gain[n : n + 1, :].astype(F32), (8, BLK))
-
-    load.wait()
-    for t in range(KEEP):
-        v = tub[:, t, :].astype(F32)
-        v = v - jnp.mean(v, axis=-1, keepdims=True)
-        var = jnp.mean(v * v, axis=-1, keepdims=True)
-        xn[t * NDP : (t + 1) * NDP, :] = (v * lax.rsqrt(var + 1e-06) * gains[0:1, :]).astype(BF16)
 
     pl.semaphore_wait(barrier, len(peers))
     for dev in near:
@@ -196,6 +186,16 @@
 
     for h in FIRST_HEADS:
         begin(h)
+
+    for n in range(width // BLK):
+        gains[:, n * BLK : (n + 1) * BLK] = jnp.broadcast_to(gain[n : n + 1, :].astype(F32), (8, BLK))
+
+    load.wait()
+    for t in range(KEEP):
+        v = tub[:, t, :].astype(F32)
+        v = v - jnp.mean(v, axis=-1, keepdims=True)
+        var = jnp.mean(v * v, axis=-1, keepdims=True)
+        xn[t * NDP : (t + 1) * NDP, :] = (v * lax.rsqrt(var + 1e-06) * gains[0:1, :]).astype(BF16)
 
     kept = [keep[e : e + 1, :] >= 0 for e in range(KEEP)]
     mine = [keep[e : e + 1, :] - j_me * KEEP for e in range(KEEP)]
@@ -308,12 +308,15 @@
         recv(nreg(far, g, 1), Y_ID[dx, "m2"])
         send(nreg(far, g), Y_ID[dx, "f2"], twin)
 
-    def y_end(dx):
-        g = wrap(x - dx, NX)
-        recv(nreg(jdx(y, 1 - c), g), Y_ID[dx, "own"])
-        recv(nreg(jdx(y - 1, 1 - c), g), Y_ID[dx, "fp1"])
-        recv(nreg(jdx(y + 1, 1 - c), g), Y_ID[dx, "fm1"])
-        recv(nreg(jdx(y + 2, 1 - c), g), Y_ID[dx, "f2"])
+    def y_twin(dx):
+        recv(nreg(jdx(y, 1 - c), wrap(x - dx, NX)), Y_ID[dx, "own"])
+
+    def y_twin_near(dx):
+        recv(nreg(jdx(y - 1, 1 - c), wrap(x - dx, NX)), Y_ID[dx, "fp1"])
+        recv(nreg(jdx(y + 1, 1 - c), wrap(x - dx, NX)), Y_ID[dx, "fm1"])
+
+    def y_twin_far(dx):
+        recv(nreg(jdx(y + 2, 1 - c), wrap(x - dx, NX)), Y_ID[dx, "f2"])
 
     def weights(name, h, *at):
         if name == "bx":
@@ -327,29 +330,46 @@
             for s in (t, -t) if t < 4 else (t,):
                 BX[h][s].begin()
 
-    def qkv_of(h, half):
-        @pl.loop(half * 2, half * 2 + 2)
-        def _(m):
-            lhs = nrm[pl.ds(m * 2, 2)].reshape(2 * BLK, NDP * BLK)
-            rhs = wall[h].reshape(NDP * BLK, 3 * HS)
-            acc = jnp.dot(lhs, rhs, preferred_element_type=F32)
-            col = iota(acc.shape, 1)
-            acc = acc * jnp.where(col < HS, HS ** (-0.5), 1.0)
-            qkv[pl.ds(m * 2, 2)] = acc.astype(BF16).reshape(2, BLK, 3 * HS)
+    def product(h, rows, xx):
+        cols = pl.ds(pl.multiple_of(xx * NZ * BLK, BLK), NZ * BLK)
+        lhs = nrm[rows, :, cols].reshape(2 * BLK, NZ * BLK)
+        rhs = wall[h, xx].reshape(NZ * BLK, 3 * HS)
+        return jnp.dot(lhs, rhs, preferred_element_type=F32)
+
+    def qkv_of(h, part, step=0):
+        if part == 0:
+            rows = pl.ds(2 * wrap(y + (0, 1, -1, 2)[step], NY), 2)
+            parts = [product(h, rows, wrap(x + d, NX)) for d in (0, 1, -1)]
+            acc[h, rows] = (parts[0] + parts[1] + parts[2]).reshape(2, BLK, 3 * HS)
+            return
+
+        for m in range(NT // 2):
+            rows = pl.ds(m * 2, 2)
+            full = acc[h, rows].reshape(2 * BLK, 3 * HS) + product(h, rows, wrap(x + 2, NX))
+            full = full * jnp.where(iota(full.shape, 1) < HS, HS ** (-0.5), 1.0)
+            qkv[h, rows] = full.astype(BF16).reshape(2, BLK, 3 * HS)
 
     def attend(h):
         for pg in range(8):
-            part = qkv[:, pg * 16 : (pg + 1) * 16, :].reshape(BLK, 3 * HS)
-            q, k, v = part[:, :HS], part[:, HS : 2 * HS], part[:, 2 * HS :]
+            part = qkv[h, :, pg * 16 : (pg + 1) * 16, : 2 * HS]
+            q, k = part[..., :HS].reshape(BLK, HS), part[..., HS:].reshape(BLK, HS)
             s = lax.dot_general(q, k, (((1,), (1,)), ((), ())), preferred_element_type=F32)
-            s = s + bias[pg]
+            score[pg] = s + bias[pg]
+        for pg in range(8):
+            s = score[pg]
             s = jnp.exp(s - jnp.max(s, axis=1, keepdims=True))
-            w = (s / jnp.sum(s, axis=1, keepdims=True)).astype(BF16)
-            o = jnp.dot(w, v, preferred_element_type=F32).astype(BF16)
-            att[:, pg * 16 : (pg + 1) * 16, h * HS : (h + 1) * HS] = o.reshape(NT, 16, HS)
+            prob[pg] = (s / jnp.sum(s, axis=1, keepdims=True)).astype(BF16)
+        for pg in range(8):
+            v = qkv[h, :, pg * 16 : (pg + 1) * 16, 2 * HS :].reshape(BLK, HS)
+            o = jnp.dot(prob[pg], v, preferred_element_type=F32).astype(BF16)
+            att[:, pg * 16 : (pg + 1) * 16, :] = o.reshape(NT, 16, HS)
+        for j in range(NT):
+            out[j * BLK : (j + 1) * BLK, h * HS : (h + 1) * HS] = jnp.dot(
+                place[j], att[j], preferred_element_type=F32
+            ).astype(BF16)
 
     acts = {
-        "yu": y_unpack, "yn": y_near, "yf": y_far, "ye": y_end, "A": exchange, "W": begin,
+        "yu": y_unpack, "yn": y_near, "yf": y_far, "y0": y_twin, "y1": y_twin_near, "y2": y_twin_far, "A": exchange, "W": begin,
         "pl": slot_order, "q": qkv_of, "t": attend,
     }
     for name, *rest in PLAN:
@@ -357,11 +377,6 @@
             acts[name](*rest)
         else:
             weights(name, *rest)
-
-    for j in range(NT):
-        out[j * BLK : (j + 1) * BLK, :] = jnp.dot(
-            place[j], att[j], preferred_element_type=F32
-        ).astype(BF16)
 
     for cp in sent:
         cp.wait_send()
@@ -388,8 +403,11 @@
             pltpu.VMEM((NDP, 16, width // 4), BF16),
             pltpu.VMEM((NT, BLK, width), BF16),
             pltpu.VMEM((HEADS, NX, NZ, BLK, 3 * HS), BF16),
-            pltpu.VMEM((NT, BLK, 3 * HS), BF16),
-            pltpu.VMEM((NT, BLK, cols), BF16),
+            pltpu.VMEM((HEADS, NT, BLK, 3 * HS), F32),
+            pltpu.VMEM((HEADS, NT, BLK, 3 * HS), BF16),
+            pltpu.VMEM((NT, BLK, HS), BF16),
+            pltpu.VMEM((8, BLK, BLK), F32),
+            pltpu.VMEM((8, BLK, BLK), BF16),
             pltpu.VMEM((8, BLK, BLK), F32),
             pltpu.VMEM((NT, BLK, BLK), BF16),
             pltpu.VMEM((NT, BLK), F32),

time: 104 us -> 97.3 us (0.936)
  Pallas kernels: 102 us -> 95 us
    pallas_call x1, Pallas kernels: 102 us -> 95 us  [body(): pl.pallas_call(kernel, out_shape=jax.ShapeDtypeStruct((NT * BLK, cols), B...]
where the time goes in v3:
time: 97.3 us; the launch traced here: 97.2 us
  Pallas kernels  95 us (98%)
  local copies, waits for them, and re-layouts  2.09 us (2%)
    pallas_call x1, Pallas kernels, body(): pl.pallas_call(kernel, out_shape=jax.ShapeDtypeStruct((NT * BLK, cols), B...  95 us
    unnamed x1, local copies, waits for them, and re-layouts  2.09 us

profile of v3, /device:TPU:16, one launch (start us, length us, event | category | flops | bytes accessed | tf_op | source)
XLA Modules:
  0.0 97.2 jit_solution(13556189381159508634)
XLA Ops:
  0.0 95.0 %repack_attend.1 = bf16[1024,384]{1,0:T(8,128)(2,1)} custom-call(bf16[32,4,4096]{2,1,0:T(4,128)(2,1)} %tub_hbm.1, s32[4,32]{1,0:T(4,128)} %bitcast.7, s32[4,32]{1,0:T(4,128)} %bitcast.8, s32[4,32]{1,0:T(4,128)} %bitcast.9, s32[1,1024]{1,0:T(1,128)} %seg.1, bf16[32,128]{1,0:T(8,128)(2,1)} %bitcast.6, bf16[128,384]{1,0:T(8,128)(2,1)} %wq.1, ...), custom_call_target="tpu_custom_call" | custom-call | tf_op jit(solution)/shard_map/repack_attend/pallas_call | solution.py:393
  95.1 2.1 %copy.11 = bf16[1,1024,384]{2,1,0:T(8,128)(2,1)} copy(bf16[1,1024,384]{2,1,0:T(8,128)(2,1)} %bitcast.5) | data formatting | bytes 1572864

commit v4 on v3

--- a/solution.py
+++ b/solution.py
@@ -34,24 +34,26 @@
 
 PLAN = (
     ("ax", 0, 1), ("bz", 0, 1), ("A", 1), ("bx", 0, 0, 1), ("ax", 1, 1), ("bz", 1, 1), ("bx", 1, 0, 1),
-    ("ax", 0, 2), ("bx", 0, 1, 1), ("bx", 0, -1, 1), ("bz", 0, 2), ("A", 3), ("bx", 0, 0, 2), ("ax", 1, 2),
-    ("yu", 0), ("A", 2), ("bx", 1, 1, 1), ("bx", 1, -1, 1), ("y0", 0), ("bx", 1, 0, 2), ("bz", 1, 2),
-    ("bx", 0, 1, 2), ("bx", 0, -1, 2), ("bx", 0, 2, 1), ("az", 0, 1), ("yn", 0), ("pl",), ("bx", 0, -2, 1),
-    ("yu", 1), ("bz", 0, 3), ("y1", 0), ("y0", 1), ("yf", 0), ("bx", 1, 1, 2), ("y2", 0), ("bx", 1, -1, 2),
-    ("bx", 1, 2, 1), ("yn", 1), ("yu", 3), ("bx", 1, -2, 1), ("bx", 0, 2, 2), ("bx", 0, -2, 2), ("y1", 1),
-    ("bx", 0, 3, 1), ("az", 1, 1), ("y0", 3), ("yf", 1), ("bx", 0, -3, 1), ("bx", 1, 2, 2), ("bz", 1, 3),
-    ("bx", 1, -2, 2), ("y2", 1), ("bx", 0, 3, 2), ("bx", 0, -3, 2), ("yu", 2), ("az", 0, 2), ("bz", 0, 4),
-    ("W", 2), ("bx", 1, 3, 1), ("yn", 3), ("y0", 2), ("bx", 1, -3, 1), ("az", 1, 2), ("bz", 1, 4),
-    ("bx", 0, 4, 1), ("ax", 2, 1), ("y1", 3), ("bx", 2, 0, 1), ("az", 0, 3), ("bx", 1, 3, 2), ("yn", 2),
-    ("bx", 1, -3, 2), ("bz", 2, 1), ("bx", 1, 4, 1), ("bx", 0, 4, 2), ("az", 1, 3), ("ax", 2, 2), ("yf", 3),
-    ("y1", 2), ("bx", 2, 0, 2), ("az", 0, 4), ("q", 0, 0, 0), ("q", 0, 0, 1), ("bx", 2, 1, 1), ("y2", 3),
-    ("bz", 2, 2), ("yf", 2), ("q", 0, 0, 2), ("bx", 2, -1, 1), ("az", 1, 4), ("q", 1, 0, 0), ("bx", 1, 4, 2),
-    ("bx", 2, 1, 2), ("y2", 2), ("q", 0, 0, 3), ("az", 2, 1), ("q", 0, 1), ("bx", 2, 2, 1), ("bz", 2, 3),
-    ("bx", 2, -2, 1), ("t", 0), ("bx", 2, -1, 2), ("q", 1, 0, 1), ("az", 2, 2), ("bx", 2, 2, 2),
-    ("q", 1, 0, 2), ("bz", 2, 4), ("q", 1, 0, 3), ("bx", 2, 3, 1), ("q", 1, 1), ("bx", 2, -3, 1), ("az", 2, 3),
-    ("bx", 2, -2, 2), ("t", 1), ("bx", 2, 4, 1), ("bx", 2, 3, 2), ("az", 2, 4), ("q", 2, 0, 0),
-    ("bx", 2, -3, 2), ("bx", 2, 4, 2), ("q", 2, 0, 1), ("q", 2, 0, 2), ("q", 2, 0, 3), ("q", 2, 1), ("t", 2),
+    ("ax", 0, 2), ("bx", 0, 1, 1), ("bx", 0, -1, 1), ("bz", 0, 2), ("A", 3), ("ax", 1, 2), ("yu", 0), ("A", 2),
+    ("bx", 1, 1, 1), ("bx", 1, -1, 1), ("bz", 1, 2), ("bx", 0, 2, 1), ("az", 0, 1), ("yn", 0), ("pl",),
+    ("bx", 0, -2, 1), ("yu", 1), ("bz", 0, 3), ("yf", 0), ("bx", 1, 2, 1), ("yn", 1), ("yu", 3),
+    ("bx", 1, -2, 1), ("bx", 0, 3, 1), ("az", 1, 1), ("yf", 1), ("bx", 0, -3, 1), ("bz", 1, 3), ("yu", 2),
+    ("az", 0, 2), ("bz", 0, 4), ("W", 2), ("bx", 1, 3, 1), ("yn", 3), ("bx", 1, -3, 1), ("az", 1, 2),
+    ("bz", 1, 4), ("bx", 0, 4, 1), ("ax", 2, 1), ("bx", 2, 0, 1), ("az", 0, 3), ("yn", 2), ("bz", 2, 1),
+    ("bx", 1, 4, 1), ("az", 1, 3), ("ax", 2, 2), ("yf", 3), ("az", 0, 4), ("y0", 0), ("y0", 1), ("y0", 3),
+    ("y0", 2), ("q", 0, 0, 0), ("y1", 0), ("y1", 1), ("y1", 3), ("y1", 2), ("q", 0, 0, 1), ("bx", 2, 1, 1),
+    ("bz", 2, 2), ("yf", 2), ("q", 0, 0, 2), ("bx", 2, -1, 1), ("az", 1, 4), ("q", 1, 0, 0), ("y2", 0),
+    ("y2", 1), ("y2", 3), ("y2", 2), ("q", 0, 0, 3), ("az", 2, 1), ("bx", 0, 0, 2), ("bx", 0, 1, 2),
+    ("bx", 0, -1, 2), ("bx", 0, 2, 2), ("bx", 0, -2, 2), ("bx", 0, 3, 2), ("bx", 0, -3, 2), ("bx", 0, 4, 2),
+    ("q", 0, 1), ("bx", 2, 2, 1), ("bz", 2, 3), ("bx", 2, -2, 1), ("t", 0), ("q", 1, 0, 1), ("az", 2, 2),
+    ("q", 1, 0, 2), ("bz", 2, 4), ("q", 1, 0, 3), ("bx", 2, 3, 1), ("bx", 1, 0, 2), ("bx", 1, 1, 2),
+    ("bx", 1, -1, 2), ("bx", 1, 2, 2), ("bx", 1, -2, 2), ("bx", 1, 3, 2), ("bx", 1, -3, 2), ("bx", 1, 4, 2),
+    ("q", 1, 1), ("bx", 2, -3, 1), ("az", 2, 3), ("t", 1), ("bx", 2, 4, 1), ("az", 2, 4), ("q", 2, 0, 0),
+    ("q", 2, 0, 1), ("q", 2, 0, 2), ("q", 2, 0, 3), ("bx", 2, 0, 2), ("bx", 2, 1, 2), ("bx", 2, -1, 2),
+    ("bx", 2, 2, 2), ("bx", 2, -2, 2), ("bx", 2, 3, 2), ("bx", 2, -3, 2), ("bx", 2, 4, 2), ("q", 2, 1),
+    ("t", 2),
 )
+
 FIRST_GROUPS, FIRST_HEADS = (0,), (0, 1)
 
 

time: 97.3 us -> 95 us (0.976)
  Pallas kernels: 95 us -> 92.7 us
    pallas_call x1, Pallas kernels: 95 us -> 92.7 us  [body(): pl.pallas_call(kernel, out_shape=jax.ShapeDtypeStruct((NT * BLK, cols), B...]
where the time goes in v4:
time: 95 us; the launch traced here: 94.8 us
  Pallas kernels  92.7 us (98%)
  local copies, waits for them, and re-layouts  2.09 us (2%)
    pallas_call x1, Pallas kernels, body(): pl.pallas_call(kernel, out_shape=jax.ShapeDtypeStruct((NT * BLK, cols), B...  92.7 us
    unnamed x1, local copies, waits for them, and re-layouts  2.09 us

profile of v4, /device:TPU:16, one launch (start us, length us, event | category | flops | bytes accessed | tf_op | source)
XLA Modules:
  0.0 94.8 jit_solution(15741566662803352296)
XLA Ops:
  0.0 92.7 %repack_attend.1 = bf16[1024,384]{1,0:T(8,128)(2,1)} custom-call(bf16[32,4,4096]{2,1,0:T(4,128)(2,1)} %tub_hbm.1, s32[4,32]{1,0:T(4,128)} %bitcast.7, s32[4,32]{1,0:T(4,128)} %bitcast.8, s32[4,32]{1,0:T(4,128)} %bitcast.9, s32[1,1024]{1,0:T(1,128)} %seg.1, bf16[32,128]{1,0:T(8,128)(2,1)} %bitcast.6, bf16[128,384]{1,0:T(8,128)(2,1)} %wq.1, ...), custom_call_target="tpu_custom_call" | custom-call | tf_op jit(solution)/shard_map/repack_attend/pallas_call | solution.py:395
  92.7 2.1 %copy.11 = bf16[1,1024,384]{2,1,0:T(8,128)(2,1)} copy(bf16[1,1024,384]{2,1,0:T(8,128)(2,1)} %bitcast.5) | data formatting | bytes 1572864
